TPU v7x, 256 devices: a whole 4x4x8 slice. The times are simulated.
256 devices in a mesh: grid: 64 (over y, z, core), rep: 4 (over x).
Axes of the slice: x: 4, y: 4, z: 8, core: 2. Of those that a mesh axis runs over, the one named last changes fastest.
Arguments:
- integrals: bfloat16 [131072, 512], P(('grid', 'rep')), may hold values from -6 to 6
- green_occ: bfloat16 [512, 16384], P(None, 'grid'), may hold values from -0.25 to 0.25
- tile_panels: int32 [1024, 16], P(('grid', 'rep')), may hold values from 0 to 63, all different within a row; in each aligned block of 4 rows (0 to 3, 4 to 7, ...) at most 2 rows name the same one
- virtual_blocks: bfloat16 [64, 16, 256, 256], P('grid', 'rep'), may hold values from -0.0234375 to 0.0234375
Outputs:
- response_blocks: float32 [64, 128, 256], P('grid', 'rep')
Inputs may be any that keep to these rules, and one draw needn't show every extreme that they name: `tile_panels`: each row lists 16 different panels. In each aligned block of 4 rows (the tiles of one device) no panel is listed by more than 2 rows, and some panel is listed by exactly 2 rows.
All inputs are finite; a program needn't handle non-finite values.
Results may differ from a plain program's by a relative error of at most 0.0029.
Values may be sent and summed in bfloat16 or wider, within the bound.
A program may use at most 128 MiB of HBM per device.

v0:
```python
import jax
import jax.numpy as jnp
from jax import lax
from jax.sharding import PartitionSpec as P

CAP = 2


def shards(integrals, green_occ, tile_panels, virtual_blocks):
    grid_count = lax.axis_size("grid")
    tile_count = tile_panels.shape[0]
    tile_rows = integrals.shape[0] // tile_count
    panel_width = green_occ.shape[1]
    owners = jnp.arange(grid_count, dtype=jnp.int32)
    hit_count = jnp.sum(
        (tile_panels[:, :, None] == owners[None, None, :]).astype(jnp.int32), axis=1
    )
    before = jnp.cumsum(hit_count, axis=0) - hit_count
    slot_ids = jnp.arange(CAP, dtype=jnp.int32)
    placement = (hit_count[:, :, None] == 1) & (before[:, :, None] == slot_ids[None, None, :])
    place_weights = placement.astype(jnp.bfloat16)
    tile_ids = jnp.arange(tile_count, dtype=jnp.int32)
    labels = jnp.sum(placement.astype(jnp.int32) * tile_ids[:, None, None], axis=0)
    contracted = jnp.dot(
        integrals,
        lax.all_gather(green_occ, "grid", axis=1, tiled=True),
        preferred_element_type=jnp.float32,
    ).astype(jnp.bfloat16)
    tile_blocks = contracted.reshape(tile_count, tile_rows, grid_count, panel_width)
    outgoing = jnp.einsum(
        "ldc,ltdw->dctw", place_weights, tile_blocks, preferred_element_type=jnp.float32
    ).astype(jnp.bfloat16)
    arrived, got_labels = (
        lax.all_to_all(outgoing, "grid", split_axis=0, concat_axis=0, tiled=True),
        lax.all_to_all(labels, "grid", split_axis=0, concat_axis=0, tiled=True),
    )
    slot_owner = (got_labels[:, :, None] == tile_ids[None, None, :]).astype(jnp.bfloat16)
    summed = jnp.einsum("gcl,gctw->ltw", slot_owner, arrived, preferred_element_type=jnp.float32)
    owner_part = jnp.einsum(
        "ltw,lwc->tc",
        summed,
        virtual_blocks[0].astype(jnp.float32),
        precision=lax.Precision.HIGHEST,
    )
    return lax.psum_scatter(owner_part[None], "rep", scatter_dimension=1, tiled=True)


def solution(mesh):
    in_specs = (
        P(("grid", "rep"), None),
        P(None, "grid"),
        P(("grid", "rep"), None),
        P("grid", "rep", None, None),
    )
    out_specs = P("grid", "rep", None)
    return jax.shard_map(shards, mesh=mesh, in_specs=in_specs, out_specs=out_specs, check_vma=False)
```

profile of v0, /device:TPU:8, one launch (start us, length us, event | category | flops | bytes accessed | tf_op | source)
XLA Modules:
  0.0 416.4 jit_solution(14238982077939714297)
XLA Ops:
  6.5 0.0 copy-start
  6.5 0.0 all-gather.2.cloned.1.call-start
  6.5 0.7 all-gather.2.cloned.1.call-update
  7.3 0.8 convert_reduce_fusion
  8.1 0.7 copy.9
  8.8 12.1 %all-to-all-start = ((s32[64,1,2]{2,1,0:T(1,128)}), s32[64,1,2]{2,1,0:T(1,128)S(1)}, u32[]{:S(2)}, u32[]{:S(2)}) async-start(s32[64,1,2]{2,1,0:T(1,128)} %copy.9), calls=%async_computation | async-start | bytes 65536 | tf_op jit(solution)/shard_map/all_to_all | solution.py:35
  21.0 0.1 copy.15
  21.1 96.2 %all-gather.2.cloned.1.call-done = bf16[512,16384]{1,0:T(8,128)(2,1)} async-done(((bf16[512,256]{1,0:T(8,128)(2,1)}), bf16[512,16384]{1,0:T(8,128)(2,1)}) %all-gather.2.cloned.1.call-update) | async-done | bytes 16777232 | tf_op jit(solution)/shard_map/all_gather | solution.py:26
  117.3 0.0 copy-done
  117.3 18.0 %convolution_convert_fusion = bf16[512,16384]{1,0:T(8,128)(2,1)} fusion(bf16[512,512]{1,0:T(8,128)(2,1)S(1)} %copy-done, bf16[512,16384]{1,0:T(8,128)(2,1)} %all-gather.2.cloned.1.call-done), kind=kOutput, calls=%fused_computation | convolution fusion | flops 8598323200 | bytes 34078720 | tf_op jit(solution)/shard_map/dot_general | solution.py:24
  135.4 10.3 %copy.19 = bf16[64,8,64,256]{3,2,1,0:T(8,128)(2,1)S(1)} copy(bf16[64,8,64,256]{3,1,2,0:T(8,128)(2,1)} %bitcast.23) | data formatting | bytes 33554432
  145.6 0.0 copy-start.1
  145.6 35.7 %fusion.2 = bf16[64,2,128,256]{3,1,2,0:T(2,128)(2,1)} fusion(pred[4,64,2,1]{0,2,3,1:T(4,128)(4,1)S(1)} %copy.15, bf16[4,128,64,256]{3,2,1,0:T(8,128)(2,1)S(1)} %bitcast.22), kind=kOutput, calls=%fused_computation.3 | convolution fusion | flops 37748736 | bytes 25166336 | tf_op jit(solution)/shard_map/ldc,ltdw->dctw/dot_general | solution.py:30
  181.4 0.0 all-to-all-done
  181.4 9.3 %all-to-all-start.1 = ((bf16[64,2,128,256]{3,1,2,0:T(2,128)(2,1)}), bf16[64,2,128,256]{3,1,2,0:T(2,128)(2,1)}, u32[]{:S(2)}, u32[]{:S(2)}) async-start(bf16[64,2,128,256]{3,1,2,0:T(2,128)(2,1)} %fusion.2), calls=%async_computation.1 | async-start | bytes 16777216 | tf_op jit(solution)/shard_map/all_to_all | solution.py:34
  190.6 0.0 reduce-scatter.2.cloned.1.call-start
  190.7 0.1 copy.10
  190.8 184.1 %all-to-all-done.1 = bf16[64,2,128,256]{3,1,2,0:T(2,128)(2,1)} async-done(((bf16[64,2,128,256]{3,1,2,0:T(2,128)(2,1)}), bf16[64,2,128,256]{3,1,2,0:T(2,128)(2,1)}, u32[]{:S(2)}, u32[]{:S(2)}) %all-to-all-start.1) | async-done | bytes 8388640 | tf_op jit(solution)/shard_map/all_to_all | solution.py:34
  374.9 12.2 %fusion.7 = f32[4,128,256]{2,0,1:T(4,128)S(1)} fusion(bf16[64,2,128,256]{3,1,2,0:T(2,128)(2,1)} %all-to-all-done.1, s32[64,2]{0,1:T(2,128)S(1)} %bitcast.24), kind=kOutput, calls=%fused_computation.6 | convolution fusion | flops 33554944 | bytes 8913408 | tf_op jit(solution)/shard_map/gcl,gctw->ltw/dot_general | solution.py:38
  387.1 0.0 copy-done.2
  387.1 1.1 convolution_bitcast_fusion
  388.2 0.0 reduce-scatter.2.cloned.1.call-update
  388.2 21.4 %reduce-scatter.2.cloned.1.call-done = f32[1,32,256]{2,1,0:T(8,128)} async-done(((f32[1,128,256]{2,1,0:T(8,128)}), f32[1,32,256]{2,1,0:T(8,128)}) %reduce-scatter.2.cloned.1.call-update) | async-done | bytes 32784 | tf_op jit(solution)/shard_map/reduce_scatter | solution.py:45
  409.6 0.0 copy-done.1
  (6 shorter events, 0.1 us)
Async XLA Ops:
  6.5 110.8 %copy-start = (bf16[512,512]{1,0:T(8,128)(2,1)S(1)}, bf16[512,512]{1,0:T(8,128)(2,1)}, u32[]{:S(2)}) copy-start(bf16[512,512]{1,0:T(8,128)(2,1)} %param.4) | copy-start | bytes 1572868
  6.5 110.8 %all-gather.2.cloned.1.call-start = ((), (), s32[]{:S(2)}) async-start(), calls=%async_computation.3 | async-start | bytes 17039360 | tf_op jit(solution)/shard_map/all_gather | solution.py:26
  8.8 172.6 %all-to-all-start = ((s32[64,1,2]{2,1,0:T(1,128)}), s32[64,1,2]{2,1,0:T(1,128)S(1)}, u32[]{:S(2)}, u32[]{:S(2)}) async-start(s32[64,1,2]{2,1,0:T(1,128)} %copy.9), calls=%async_computation | async-start | bytes 65536 | tf_op jit(solution)/shard_map/all_to_all | solution.py:35
  145.6 264.0 %copy-start.1 = (bf16[512,512]{1,0:T(8,128)(2,1)S(1)}, bf16[512,512]{1,0:T(8,128)(2,1)}, u32[]{:S(2)}) copy-start(bf16[512,512]{1,0:T(8,128)(2,1)} %param.4) | copy-start | bytes 1572868
  181.4 205.7 %copy-start.2 = (bf16[1,4,256,256]{3,2,1,0:T(8,128)(2,1)S(1)}, bf16[1,4,256,256]{3,2,1,0:T(8,128)(2,1)}, u32[]{:S(2)}) copy-start(bf16[1,4,256,256]{3,2,1,0:T(8,128)(2,1)} %param.7) | copy-start | bytes 1572868
  181.4 193.5 %all-to-all-start.1 = ((bf16[64,2,128,256]{3,1,2,0:T(2,128)(2,1)}), bf16[64,2,128,256]{3,1,2,0:T(2,128)(2,1)}, u32[]{:S(2)}, u32[]{:S(2)}) async-start(bf16[64,2,128,256]{3,1,2,0:T(2,128)(2,1)} %fusion.2), calls=%async_computation.1 | async-start | bytes 16777216 | tf_op jit(solution)/shard_map/all_to_all | solution.py:34
  190.6 218.9 %reduce-scatter.2.cloned.1.call-start = ((), (), s32[]{:S(2)}) async-start(), calls=%async_computation.4 | async-start | bytes 163840 | tf_op jit(solution)/shard_map/reduce_scatter | solution.py:45
Sparse Core Ops, SparseCore 0:
  9.9 107.3 all-gather.1
  388.3 21.1 reduce-scatter.1
where the time goes:
time: 417 us; the launch traced here: 416 us
  waiting for transfers between devices  302 us (72%)
  matrix products  67.1 us (16%)
  starting transfers between devices  21.4 us (5%)
  between operations  13.5 us (3%)
  local copies, waits for them, and re-layouts  11.2 us (3%)
    all_to_all x1, waiting for transfers between devices, shards(): lax.all_to_all(outgoing, 'grid', split_axis=0, concat_axis=0, tiled=True)  184 us
    all_gather x1, waiting for transfers between devices, shards(): lax.all_gather(green_occ, 'grid', axis=1, tiled=True)  96.2 us
    dot_general x1, matrix products, shards(): jnp.einsum('ldc,ltdw->dctw', place_weights, tile_blocks, preferred_elemen...  35.7 us
    reduce_scatter x1, waiting for transfers between devices, shards(): lax.psum_scatter(owner_part[None], 'rep', scatter_dimension=1, tiled=True)  21.4 us
    dot_general x1, matrix products, shards(): jnp.dot(integrals, lax.all_gather(green_occ, 'grid', axis=1, tiled=True),...  18 us
    dot_general x1, matrix products, shards(): jnp.einsum('gcl,gctw->ltw', slot_owner, arrived, preferred_element_type=j...  12.2 us
    all_to_all x1, starting transfers between devices, shards(): lax.all_to_all(labels, 'grid', split_axis=0, concat_axis=0, tiled=True)  12.1 us
    unnamed x7, local copies, waits for them, and re-layouts  10.3 us
  transfers between devices with their start and end apart: 4, of which 3 were waited for; matrix products, arithmetic and copies ran while one was open for 16% of the time, Pallas kernels for 0%

commit v1 on v0

--- a/solution.py
+++ b/solution.py
@@ -23,7 +23,15 @@
     labels = jnp.sum(placement.astype(jnp.int32) * tile_ids[:, None, None], axis=0)
     contracted = jnp.dot(
         integrals,
-        lax.all_gather(green_occ, "grid", axis=1, tiled=True),
+        jnp.concatenate(
+            jax.lax.all_to_all(
+                jnp.stack(jax.lax.axis_size("grid") * [green_occ], axis=0),
+                concat_axis=0,
+                split_axis=0,
+                axis_name="grid",
+            ),
+            axis=1,
+        ),
         preferred_element_type=jnp.float32,
     ).astype(jnp.bfloat16)
     tile_blocks = contracted.reshape(tile_count, tile_rows, grid_count, panel_width)

time: 417 us -> 691 us (1.66)
  waiting for transfers between devices: 302 us -> 569 us
  starting transfers between devices: 21.4 us -> 29.3 us
  matrix products: 67.1 us -> 59.3 us
    all_to_all x0 -> x1, waiting for transfers between devices: none -> 363 us  [shards(): jax.lax.all_to_all(jnp.stack(jax.lax.axis_size('grid') * [green_occ], axi...]
    all_gather x1 -> x0, waiting for transfers between devices: 96.2 us -> none  [shards(): lax.all_gather(green_occ, 'grid', axis=1, tiled=True)]
    all_to_all x0 -> x1, starting transfers between devices: none -> 12.4 us  [shards(): jax.lax.all_to_all(jnp.stack(jax.lax.axis_size('grid') * [green_occ], axi...]
    dot_general x1, matrix products: 35.7 us -> 27.2 us  [shards(): jnp.einsum('ldc,ltdw->dctw', place_weights, tile_blocks, preferred_elemen...]
  transfers between devices with their start and end apart: 4 -> 4, of which waited for: 3 -> 3; matrix products, arithmetic and copies ran while one was open for 16% -> 8% of each run, Pallas kernels for 0% -> 0%
where the time goes in v1:
time: 691 us; the launch traced here: 690 us
  waiting for transfers between devices  569 us (82%)
  matrix products  59.3 us (9%)
  starting transfers between devices  29.3 us (4%)
  local copies, waits for them, and re-layouts  17.7 us (3%)
  between operations  13.5 us (2%)
    all_to_all x1, waiting for transfers between devices, shards(): jax.lax.all_to_all(jnp.stack(jax.lax.axis_size('grid') * [green_occ], axi...  363 us
    all_to_all x1, waiting for transfers between devices, shards(): lax.all_to_all(outgoing, 'grid', split_axis=0, concat_axis=0, tiled=True)  184 us
    dot_general x1, matrix products, shards(): jnp.einsum('ldc,ltdw->dctw', place_weights, tile_blocks, preferred_elemen...  27.2 us
    reduce_scatter x1, waiting for transfers between devices, shards(): lax.psum_scatter(owner_part[None], 'rep', scatter_dimension=1, tiled=True)  21.4 us
    dot_general x1, matrix products, shards(): jnp.dot(integrals, jnp.concatenate(jax.lax.all_to_all(jnp.stack(jax.lax.a...  18.9 us
  transfers between devices with their start and end apart: 4, of which 3 were waited for; matrix products, arithmetic and copies ran while one was open for 8% of the time, Pallas kernels for 0%

profile of v1, /device:TPU:8, one launch (start us, length us, event | category | flops | bytes accessed | tf_op | source)
XLA Modules:
  0.0 690.2 jit_solution(9280723597258465777)
XLA Ops:
  6.5 0.0 copy-start
  6.5 1.1 copy.26
  7.7 6.0 stack.2
  13.7 12.4 %all-to-all-start.1 = ((bf16[64,512,256]{1,2,0:T(8,128)(2,1)}), bf16[64,512,256]{1,2,0:T(8,128)(2,1)}, u32[]{:S(2)}, u32[]{:S(2)}) async-start(bf16[64,512,256]{1,2,0:T(8,128)(2,1)} %stack.2), calls=%async_computation.1 | async-start | bytes 33554432 | tf_op jit(solution)/shard_map/all_to_all | solution.py:27
  26.1 0.0 copy-done.3
  26.1 0.1 convert_reduce_fusion
  26.2 0.1 copy.21
  26.4 0.1 copy.22
  26.5 1.8 select_reduce_fusion
  28.3 363.0 %all-to-all-done.1 = bf16[64,512,256]{1,2,0:T(8,128)(2,1)} async-done(((bf16[64,512,256]{1,2,0:T(8,128)(2,1)}), bf16[64,512,256]{1,2,0:T(8,128)(2,1)}, u32[]{:S(2)}, u32[]{:S(2)}) %all-to-all-start.1) | async-done | bytes 16777248 | tf_op jit(solution)/shard_map/all_to_all | solution.py:27
  391.2 6.2 all-to-all-start
  397.4 18.9 %convolution_convert_fusion = bf16[512,16384]{1,0:T(8,128)(2,1)} fusion(bf16[512,512]{1,0:T(8,128)(2,1)S(1)} %copy-done, bf16[512,16384]{0,1:T(8,128)(2,1)} %bitcast.6), kind=kOutput, calls=%fused_computation | convolution fusion | flops 8598323200 | bytes 34078720 | tf_op jit(solution)/shard_map/dot_general | solution.py:24
  416.3 10.3 %copy.34 = bf16[64,8,64,256]{3,2,1,0:T(8,128)(2,1)S(1)} copy(bf16[64,8,64,256]{3,1,2,0:T(8,128)(2,1)} %bitcast.30) | data formatting | bytes 33554432
  426.6 0.0 copy-start.1
  426.6 27.2 %fusion.2 = bf16[64,2,128,256]{3,1,2,0:T(2,128)(2,1)} fusion(bf16[4,128,64,256]{3,2,1,0:T(8,128)(2,1)S(1)} %bitcast.29, pred[4,64]{0,1:T(8,128)(4,1)S(1)} %copy.21, s32[4,64]{0,1:T(8,128)S(1)} %copy.22), kind=kOutput, calls=%fused_computation.3 | convolution fusion | flops 37749760 | bytes 25167104 | tf_op jit(solution)/shard_map/ldc,ltdw->dctw/dot_general | solution.py:38
  453.7 0.0 all-to-all-done
  453.7 10.6 %all-to-all-start.2 = ((bf16[64,2,128,256]{3,1,2,0:T(2,128)(2,1)}), bf16[64,2,128,256]{3,1,2,0:T(2,128)(2,1)}, u32[]{:S(2)}, u32[]{:S(2)}) async-start(bf16[64,2,128,256]{3,1,2,0:T(2,128)(2,1)} %fusion.2), calls=%async_computation.2 | async-start | bytes 16777216 | tf_op jit(solution)/shard_map/all_to_all | solution.py:42
  464.4 0.0 reduce-scatter.2.cloned.1.call-start
  464.4 0.1 copy.25
  464.5 184.1 %all-to-all-done.2 = bf16[64,2,128,256]{3,1,2,0:T(2,128)(2,1)} async-done(((bf16[64,2,128,256]{3,1,2,0:T(2,128)(2,1)}), bf16[64,2,128,256]{3,1,2,0:T(2,128)(2,1)}, u32[]{:S(2)}, u32[]{:S(2)}) %all-to-all-start.2) | async-done | bytes 8388640 | tf_op jit(solution)/shard_map/all_to_all | solution.py:42
  648.6 12.2 %fusion.7 = f32[4,128,256]{2,0,1:T(4,128)S(1)} fusion(bf16[64,2,128,256]{3,1,2,0:T(2,128)(2,1)} %all-to-all-done.2, s32[64,2]{0,1:T(2,128)S(1)} %bitcast.31), kind=kOutput, calls=%fused_computation.6 | convolution fusion | flops 33554944 | bytes 8913408 | tf_op jit(solution)/shard_map/gcl,gctw->ltw/dot_general | solution.py:46
  660.9 1.1 convolution_bitcast_fusion
  661.9 0.0 reduce-scatter.2.cloned.1.call-update
  662.0 21.4 %reduce-scatter.2.cloned.1.call-done = f32[1,32,256]{2,1,0:T(8,128)} async-done(((f32[1,128,256]{2,1,0:T(8,128)}), f32[1,32,256]{2,1,0:T(8,128)}) %reduce-scatter.2.cloned.1.call-update) | async-done | bytes 32784 | tf_op jit(solution)/shard_map/reduce_scatter | solution.py:53
  (8 shorter events, 0.1 us)
Async XLA Ops:
  6.5 390.9 %copy-start = (bf16[512,512]{1,0:T(8,128)(2,1)S(1)}, bf16[512,512]{1,0:T(8,128)(2,1)}, u32[]{:S(2)}) copy-start(bf16[512,512]{1,0:T(8,128)(2,1)} %param.4) | copy-start | bytes 1572868
  13.7 12.4 %copy-start.3 = (s32[4,16]{1,0:T(4,128)S(1)}, s32[4,16]{1,0:T(4,128)}, u32[]{:S(2)}) copy-start(s32[4,16]{1,0:T(4,128)} %param.6) | copy-start | bytes 772
  13.7 377.6 %all-to-all-start.1 = ((bf16[64,512,256]{1,2,0:T(8,128)(2,1)}), bf16[64,512,256]{1,2,0:T(8,128)(2,1)}, u32[]{:S(2)}, u32[]{:S(2)}) async-start(bf16[64,512,256]{1,2,0:T(8,128)(2,1)} %stack.2), calls=%async_computation.1 | async-start | bytes 33554432 | tf_op jit(solution)/shard_map/all_to_all | solution.py:27
  391.2 62.5 %all-to-all-start = ((s32[64,1,2]{2,1,0:T(1,128)}), s32[64,1,2]{2,1,0:T(1,128)S(1)}, u32[]{:S(2)}, u32[]{:S(2)}) async-start(s32[64,1,2]{2,1,0:T(1,128)} %bitcast.12), calls=%async_computation | async-start | bytes 65536 | tf_op jit(solution)/shard_map/all_to_all | solution.py:43
  426.6 256.8 %copy-start.1 = (bf16[512,512]{1,0:T(8,128)(2,1)S(1)}, bf16[512,512]{1,0:T(8,128)(2,1)}, u32[]{:S(2)}) copy-start(bf16[512,512]{1,0:T(8,128)(2,1)} %param.4) | copy-start | bytes 1572868
  453.7 207.1 %copy-start.2 = (bf16[1,4,256,256]{3,2,1,0:T(8,128)(2,1)S(1)}, bf16[1,4,256,256]{3,2,1,0:T(8,128)(2,1)}, u32[]{:S(2)}) copy-start(bf16[1,4,256,256]{3,2,1,0:T(8,128)(2,1)} %param.7) | copy-start | bytes 1572868
  453.7 194.9 %all-to-all-start.2 = ((bf16[64,2,128,256]{3,1,2,0:T(2,128)(2,1)}), bf16[64,2,128,256]{3,1,2,0:T(2,128)(2,1)}, u32[]{:S(2)}, u32[]{:S(2)}) async-start(bf16[64,2,128,256]{3,1,2,0:T(2,128)(2,1)} %fusion.2), calls=%async_computation.2 | async-start | bytes 16777216 | tf_op jit(solution)/shard_map/all_to_all | solution.py:42
  464.4 219.0 %reduce-scatter.2.cloned.1.call-start = ((), (), s32[]{:S(2)}) async-start(), calls=%async_computation.4 | async-start | bytes 163840 | tf_op jit(solution)/shard_map/reduce_scatter | solution.py:53
Sparse Core Ops, SparseCore 0:
  662.1 21.2 reduce-scatter.1
